TPU v7x, 32 devices: a whole 2x2x4 slice. The times are simulated.
32 devices in a mesh: fsdp: 8 (over z, y), ep: 4 (over x, core).
Axes of the slice: x: 2, y: 2, z: 4, core: 2. Of those that a mesh axis runs over, the one named last changes fastest.
Arguments:
- tokens: bfloat16 [4096, 3072], P(('fsdp', 'ep')), may hold values from -6 to 6
- expert_ids: int32 [4096, 2], P(('fsdp', 'ep')), may hold values from 0 to 3, all different within a row; in each aligned block of 128 rows (0 to 127, 128 to 255, ...) at most 128 rows name the same one
- gates: float32 [4096, 2], P(('fsdp', 'ep')), may hold values from 0.2 to 1
- up_weight: bfloat16 [4, 3072, 768], P('ep', 'fsdp'), may hold values from -0.109375 to 0.109375
- down_weight: bfloat16 [4, 768, 3072], P('ep', 'fsdp'), may hold values from -0.21875 to 0.21875
- cotangent: bfloat16 [4096, 3072], P(('fsdp', 'ep')), may hold values from -6 to 6
Outputs:
- mixed: bfloat16 [4096, 3072], P(('fsdp', 'ep'))
- token_grad: bfloat16 [4096, 3072], P(('fsdp', 'ep'))
- up_grad: bfloat16 [4, 3072, 768], P('ep', 'fsdp')
- down_grad: bfloat16 [4, 768, 3072], P('ep', 'fsdp')
Inputs may be any that keep to these rules, and one draw needn't show every extreme that they name: `expert_ids`: each token names two different experts. Among the tokens of one device (aligned blocks of 128 tokens) no expert is named more than 128 times, and in some block one expert is named exactly 128 times.
All inputs are finite; a program needn't handle non-finite values.
Results may differ from a plain program's by a relative error of at most 0.012.
Values may be sent and summed in bfloat16 or wider, within the bound.
A program may use at most 128 MiB of HBM per device.

v0:
```python
import jax
import jax.numpy as jnp
from jax import lax
from jax.sharding import PartitionSpec as P


def gelu_parts(pre):
    root = 0.7978845608028654
    inner = root * (pre + 0.044715 * pre * pre * pre)
    tanh_val = jnp.tanh(inner)
    value = 0.5 * pre * (1.0 + tanh_val)
    slope = 0.5 * (1.0 + tanh_val) + 0.5 * pre * (1.0 - tanh_val * tanh_val) * root * (
        1.0 + 3.0 * 0.044715 * pre * pre
    )
    return (value, slope)


def contract_last(left, right):
    return lax.dot_general(
        left, right, (((1,), (1,)), ((), ())), preferred_element_type=jnp.float32
    )


def contract_first(left, right):
    return lax.dot_general(
        left, right, (((0,), (0,)), ((), ())), preferred_element_type=jnp.float32
    )


def body(tokens, expert_ids, gates, up_weight, down_weight, cotangent):
    n_ep = lax.axis_size("ep")
    f32 = jnp.float32
    bf16 = jnp.bfloat16
    chosen = expert_ids[:, :, None] == jnp.arange(n_ep, dtype=jnp.int32)[None, None, :]
    dense_gates = jnp.sum(jnp.where(chosen, gates[:, :, None], 0.0), axis=1)
    all_gates = lax.all_gather(dense_gates, "ep", axis=0, tiled=True)
    mine = lax.axis_index("ep") == jnp.arange(n_ep, dtype=jnp.int32)
    gate = jnp.sum(jnp.where(mine[None, :], all_gates, 0.0), axis=1, keepdims=True)
    rows = lax.all_gather(tokens, "ep", axis=0, tiled=True)
    up = lax.all_gather(up_weight, "fsdp", axis=1, tiled=True)[0]
    cot = lax.all_gather(cotangent, "ep", axis=0, tiled=True)
    down = lax.all_gather(down_weight, "fsdp", axis=1, tiled=True)[0]
    grad_rows = (cot.astype(f32) * gate).astype(bf16)
    pre = jnp.dot(rows, up, preferred_element_type=f32)
    value, slope = gelu_parts(pre)
    hidden = value.astype(bf16)
    down_grad = lax.psum_scatter(
        contract_first(hidden, grad_rows).astype(bf16), "fsdp", scatter_dimension=0, tiled=True
    )
    d_hidden = contract_last(grad_rows, down)
    d_pre = (d_hidden * slope).astype(bf16)
    up_grad = lax.psum_scatter(
        contract_first(rows, d_pre).astype(bf16), "fsdp", scatter_dimension=0, tiled=True
    )
    result = jnp.dot(hidden, down, preferred_element_type=f32)
    mixed = lax.psum_scatter((result * gate).astype(bf16), "ep", scatter_dimension=0, tiled=True)
    back = contract_last(d_pre, up).astype(bf16)
    token_grad = lax.psum_scatter(back, "ep", scatter_dimension=0, tiled=True)
    return (mixed, token_grad, up_grad[None], down_grad[None])


def solution(mesh):
    placed = (
        P(("fsdp", "ep"), None),
        P(("fsdp", "ep"), None),
        P(("fsdp", "ep"), None),
        P("ep", "fsdp", None),
        P("ep", "fsdp", None),
        P(("fsdp", "ep"), None),
    )
    return jax.shard_map(
        body,
        mesh=mesh,
        in_specs=placed,
        out_specs=(
            P(("fsdp", "ep"), None),
            P(("fsdp", "ep"), None),
            P("ep", "fsdp", None),
            P("ep", "fsdp", None),
        ),
        check_vma=False,
    )
```

profile of v0, /device:TPU:0, one launch (start us, length us, event | category | flops | bytes accessed | tf_op | source)
XLA Modules:
  0.0 534.1 jit_solution(15591842795536665031)
XLA Ops:
  7.2 0.7 all-gather.5.cloned.1.call-update
  7.9 0.0 all-gather.7.cloned.1.call-start
  8.0 0.7 all-gather.7.cloned.1.call-update
  8.7 0.7 all-gather.11.cloned.1.call-update
  9.5 0.5 all-gather.9.cloned.1.call-update
  10.0 0.0 reduce-scatter.13.cloned.1.call-start
  10.1 6.1 %all_gather.18 = f32[512,4]{0,1:T(4,128)S(1)} all-gather(f32[128,4]{0,1:T(4,128)S(1)} %select_reduce_fusion.1), channel_id=1, replica_groups=mesh['fsdp'=8,'ep'=4] {'ep'}, dimensions={0}, use_global_device_ids=true | all-gather | bytes 10240 | tf_op jit(solution)/shard_map/all_gather | solution.py:36
  16.2 0.1 select_reduce_fusion
  16.3 24.6 %all-gather.5.cloned.1.call-done = bf16[512,3072]{1,0:T(8,128)(2,1)} async-done(((bf16[128,3072]{1,0:T(8,128)(2,1)}), bf16[512,3072]{1,0:T(8,128)(2,1)}) %all-gather.5.cloned.1.call-update) | async-done | bytes 3145744 | tf_op jit(solution)/shard_map/all_gather | solution.py:39
  40.8 82.1 %all-gather.7.cloned.1.call-done = bf16[1,3072,768]{2,1,0:T(8,128)(2,1)} async-done(((bf16[1,384,768]{2,1,0:T(8,128)(2,1)}), bf16[1,3072,768]{2,1,0:T(8,128)(2,1)}) %all-gather.7.cloned.1.call-update) | async-done | bytes 4718608 | tf_op jit(solution)/shard_map/all_gather | solution.py:40
  122.9 7.1 %fusion.5 = f32[512,768]{1,0:T(8,128)} fusion(bf16[512,3072]{1,0:T(8,128)(2,1)} %all-gather.5.cloned.1.call-done, bf16[1,3072,768]{2,1,0:T(8,128)(2,1)} %all-gather.7.cloned.1.call-done), kind=kOutput, calls=%fused_computation.9 | convolution fusion | flops 2415919104 | bytes 9437184 | tf_op jit(solution)/shard_map/dot_general | solution.py:44
  130.0 21.2 %all-gather.11.cloned.1.call-done = bf16[512,3072]{1,0:T(8,128)(2,1)} async-done(((bf16[128,3072]{1,0:T(8,128)(2,1)}), bf16[512,3072]{1,0:T(8,128)(2,1)}) %all-gather.11.cloned.1.call-update) | async-done | bytes 3145744 | tf_op jit(solution)/shard_map/all_gather | solution.py:41
  151.2 82.0 %all-gather.9.cloned.1.call-done = bf16[1,768,3072]{2,1,0:T(8,128)(2,1)} async-done(((bf16[1,96,3072]{2,1,0:T(8,128)(2,1)}), bf16[1,768,3072]{2,1,0:T(8,128)(2,1)}) %all-gather.9.cloned.1.call-update) | async-done | bytes 4718608 | tf_op jit(solution)/shard_map/all_gather | solution.py:42
  233.2 7.0 %fusion.17 = bf16[512,768]{1,0:T(8,128)(2,1)S(1)} fusion(f32[512,768]{1,0:T(8,128)} %fusion.5, bf16[1,768,3072]{2,1,0:T(8,128)(2,1)} %all-gather.9.cloned.1.call-done, bf16[512,3072]{1,0:T(8,128)(2,1)} %all-gather.11.cloned.1.call-done, f32[512]{0:T(512)S(1)} %select_reduce_fusion), kind=kOutput, calls=%fused_computation.21 | convolution fusion | flops 2428108800 | bytes 10225664 | tf_op jit(solution)/shard_map/dot_general | solution.py:19
  240.2 0.9 copy-done.5
  241.1 4.3 fusion.7
  245.4 6.7 %copy.17 = bf16[3072,768]{1,0:T(8,128)(2,1)} copy(bf16[3072,768]{0,1:T(8,128)(2,1)} %fusion.7) | data formatting | bytes 9437184
  252.2 0.0 reduce-scatter.7.cloned.1.call-start
  252.2 1.3 copy-done.4
  253.6 6.5 %multiply_convert_fusion.1 = bf16[512,3072]{1,0:T(8,128)(2,1)} fusion(bf16[1,768,3072]{2,1,0:T(8,128)(2,1)} %all-gather.9.cloned.1.call-done, f32[512]{0:T(512)S(1)} %select_reduce_fusion, f32[512,768]{1,0:T(8,128)S(1)} %copy-done.4), kind=kOutput, calls=%fused_computation.1 | convolution fusion | flops 2422603776 | bytes 9439232 | tf_op jit(solution)/shard_map/dot_general | solution.py:55
  260.0 0.0 reduce-scatter.9.cloned.1.call-start
  260.1 1.1 copy-done.6
  261.1 6.4 %fusion.8 = bf16[512,3072]{1,0:T(8,128)(2,1)} fusion(bf16[512,768]{1,0:T(8,128)(2,1)S(1)} %copy-done.6, bf16[1,3072,768]{2,1,0:T(8,128)(2,1)} %all-gather.7.cloned.1.call-done), kind=kOutput, calls=%fused_computation.12 | convolution fusion | flops 2417491968 | bytes 8650752 | tf_op jit(solution)/shard_map/dot_general | solution.py:19
  267.6 0.0 reduce-scatter.11.cloned.1.call-start
  267.6 1.8 copy-done.2
  269.5 6.5 %convolution_convert_fusion = bf16[768,3072]{1,0:T(8,128)(2,1)} fusion(bf16[512,3072]{1,0:T(8,128)(2,1)S(1)} %copy-done.2, f32[512]{0:T(512)S(1)} %select_reduce_fusion, f32[512,768]{1,0:T(8,128)} %fusion.5), kind=kOutput, calls=%fused_computation.2 | convolution fusion | flops 2426535936 | bytes 9439232 | tf_op jit(solution)/shard_map/dot_general | solution.py:25
  276.0 69.8 %reduce-scatter.13.cloned.1.call-done = bf16[384,768]{1,0:T(8,128)(2,1)} async-done(((bf16[3072,768]{1,0:T(8,128)(2,1)}), bf16[384,768]{1,0:T(8,128)(2,1)}) %reduce-scatter.13.cloned.1.call-update) | async-done | bytes 589840
  345.7 1.4 copy.18
  347.1 1.1 copy.16
  348.2 38.3 %reduce-scatter.7.cloned.1.call-done = bf16[128,3072]{1,0:T(8,128)(2,1)} async-done(((bf16[512,3072]{1,0:T(8,128)(2,1)}), bf16[128,3072]{1,0:T(8,128)(2,1)}) %reduce-scatter.7.cloned.1.call-update) | async-done | bytes 786448 | tf_op jit(solution)/shard_map/reduce_scatter | solution.py:56
  386.4 41.2 %reduce-scatter.9.cloned.1.call-done = bf16[128,3072]{1,0:T(8,128)(2,1)} async-done(((bf16[512,3072]{1,0:T(8,128)(2,1)}), bf16[128,3072]{1,0:T(8,128)(2,1)}) %reduce-scatter.9.cloned.1.call-update) | async-done | bytes 786448 | tf_op jit(solution)/shard_map/reduce_scatter | solution.py:58
  427.6 99.7 %reduce-scatter.11.cloned.1.call-done = bf16[96,3072]{1,0:T(8,128)(2,1)} async-done(((bf16[768,3072]{1,0:T(8,128)(2,1)}), bf16[96,3072]{1,0:T(8,128)(2,1)}) %reduce-scatter.11.cloned.1.call-update) | async-done | bytes 589840 | tf_op jit(solution)/shard_map/reduce_scatter | solution.py:47
  (19 shorter events, 0.2 us)
Async XLA Ops:
  7.2 2.9 copy-start
  7.2 2.9 copy-start.1
  7.2 33.7 %all-gather.5.cloned.1.call-start = ((), (), s32[]{:S(2)}) async-start(), calls=%async_computation.4 | async-start | bytes 3932160 | tf_op jit(solution)/shard_map/all_gather | solution.py:39
  7.9 115.0 %all-gather.7.cloned.1.call-start = ((), (), s32[]{:S(2)}) async-start(), calls=%async_computation.5 | async-start | bytes 5308416 | tf_op jit(solution)/shard_map/all_gather | solution.py:40
  8.7 142.5 %all-gather.11.cloned.1.call-start = ((), (), s32[]{:S(2)}) async-start(), calls=%async_computation.8 | async-start | bytes 3932160 | tf_op jit(solution)/shard_map/all_gather | solution.py:41
  9.4 223.8 %all-gather.9.cloned.1.call-start = ((), (), s32[]{:S(2)}) async-start(), calls=%async_computation.6 | async-start | bytes 5308416 | tf_op jit(solution)/shard_map/all_gather | solution.py:42
  10.0 335.7 %reduce-scatter.13.cloned.1.call-start = ((), (), s32[]{:S(2)}) async-start(), calls=%async_computation.11 | async-start | bytes 5308416
  130.0 111.0 %copy-start.3 = (bf16[512,3072]{1,0:T(8,128)(2,1)S(1)}, bf16[512,3072]{1,0:T(8,128)(2,1)}, u32[]{:S(2)}) copy-start(bf16[512,3072]{1,0:T(8,128)(2,1)} %all-gather.5.cloned.1.call-done) | copy-start | bytes 9437188
  240.2 0.9 copy-start.5
  252.1 1.4 copy-start.4
  252.2 134.2 %reduce-scatter.7.cloned.1.call-start = ((), (), s32[]{:S(2)}) async-start(), calls=%async_computation.7 | async-start | bytes 3932160 | tf_op jit(solution)/shard_map/reduce_scatter | solution.py:56
  260.0 1.1 copy-start.6
  260.0 167.6 %reduce-scatter.9.cloned.1.call-start = ((), (), s32[]{:S(2)}) async-start(), calls=%async_computation.9 | async-start | bytes 3932160 | tf_op jit(solution)/shard_map/reduce_scatter | solution.py:58
  267.5 1.9 copy-start.2
  267.6 259.7 %reduce-scatter.11.cloned.1.call-start = ((), (), s32[]{:S(2)}) async-start(), calls=%async_computation.10 | async-start | bytes 5308416 | tf_op jit(solution)/shard_map/reduce_scatter | solution.py:47
Sparse Core Ops, SparseCore 0:
  9.6 31.2 all-gather.4
  43.0 79.8 all-gather.6
  124.5 26.6 all-gather.10
  153.3 79.8 all-gather.8
  252.3 93.3 reduce-scatter.12
  348.7 37.6 reduce-scatter.6
  389.7 37.9 reduce-scatter.8
  431.9 95.3 reduce-scatter.10
where the time goes:
time: 535 us; the launch traced here: 534 us
  waiting for transfers between devices  461 us (86%)
  matrix products  37.8 us (7%)
  local copies, waits for them, and re-layouts  14.3 us (3%)
  between operations  14.2 us (3%)
  blocking collectives  6.11 us (1%)
    reduce_scatter x1, waiting for transfers between devices, body(): lax.psum_scatter(contract_first(hidden, grad_rows).astype(bf16), 'fsdp',...  99.7 us
    all_gather x1, waiting for transfers between devices, body(): up = lax.all_gather(up_weight, 'fsdp', axis=1, tiled=True)[0]  82.1 us
    all_gather x1, waiting for transfers between devices, body(): down = lax.all_gather(down_weight, 'fsdp', axis=1, tiled=True)[0]  82 us
    unnamed x9, waiting for transfers between devices  72.4 us
    reduce_scatter x1, waiting for transfers between devices, body(): token_grad = lax.psum_scatter(back, 'ep', scatter_dimension=0, tiled=True)  41.2 us
    reduce_scatter x1, waiting for transfers between devices, body(): lax.psum_scatter((result * gate).astype(bf16), 'ep', scatter_dimension=0,...  38.3 us
    all_gather x1, waiting for transfers between devices, body(): rows = lax.all_gather(tokens, 'ep', axis=0, tiled=True)  24.6 us
    all_gather x1, waiting for transfers between devices, body(): cot = lax.all_gather(cotangent, 'ep', axis=0, tiled=True)  21.2 us
  transfers between devices with their start and end apart: 8, of which 8 were waited for; matrix products, arithmetic and copies ran while one was open for 5% of the time, Pallas kernels for 0%

commit v1 on v0

--- a/solution.py
+++ b/solution.py
@@ -2,6 +2,27 @@
 import jax.numpy as jnp
 from jax import lax
 from jax.sharding import PartitionSpec as P
+
+
+def ring_gather(shard, axis, dim):
+    length, index, width = (lax.axis_size(axis), lax.axis_index(axis), shard.shape[dim])
+    right = [(i, (i + 1) % length) for i in range(length)]
+    behind = [(i, (i - 1) % length) for i in range(length)]
+    whole = jnp.zeros((*shard.shape[:dim], length * width, *shard.shape[dim + 1 :]), shard.dtype)
+    whole = lax.dynamic_update_slice_in_dim(whole, shard, index * width, axis=dim)
+    from_left = from_right = shard
+    half = length // 2
+    for step in range(1, half + 1):
+        from_left = lax.ppermute(from_left, axis, right)
+        whole = lax.dynamic_update_slice_in_dim(
+            whole, from_left, (index - step) % length * width, axis=dim
+        )
+        if step < length - half:
+            from_right = lax.ppermute(from_right, axis, behind)
+            whole = lax.dynamic_update_slice_in_dim(
+                whole, from_right, (index + step) % length * width, axis=dim
+            )
+    return whole
 
 
 def gelu_parts(pre):
@@ -36,7 +57,7 @@
     all_gates = lax.all_gather(dense_gates, "ep", axis=0, tiled=True)
     mine = lax.axis_index("ep") == jnp.arange(n_ep, dtype=jnp.int32)
     gate = jnp.sum(jnp.where(mine[None, :], all_gates, 0.0), axis=1, keepdims=True)
-    rows = lax.all_gather(tokens, "ep", axis=0, tiled=True)
+    rows = ring_gather(tokens, "ep", 0)
     up = lax.all_gather(up_weight, "fsdp", axis=1, tiled=True)[0]
     cot = lax.all_gather(cotangent, "ep", axis=0, tiled=True)
     down = lax.all_gather(down_weight, "fsdp", axis=1, tiled=True)[0]

time: 535 us -> 489 us (0.914)
  waiting for transfers between devices: 461 us -> 408 us
  blocking collectives: 6.11 us -> 18.4 us
  local copies, waits for them, and re-layouts: 14.3 us -> 6.11 us
    reduce_scatter x0 -> x1, waiting for transfers between devices: none -> 99.5 us  [body(): lax.psum_scatter(contract_first(rows, d_pre).astype(bf16), 'fsdp', scatte...]
    unnamed x9 -> x7, waiting for transfers between devices: 72.4 us -> 2.12 us
    all_gather x1, waiting for transfers between devices: 82.1 us -> 49 us  [body(): up = lax.all_gather(up_weight, 'fsdp', axis=1, tiled=True)[0]]
    reduce_scatter x1, waiting for transfers between devices: 38.3 us -> 12.1 us  [body(): lax.psum_scatter((result * gate).astype(bf16), 'ep', scatter_dimension=0,...]
    all_gather x1 -> x0, waiting for transfers between devices: 24.6 us -> none  [body(): rows = lax.all_gather(tokens, 'ep', axis=0, tiled=True)]
    all_gather x1, blocking collectives: 6.11 us -> 18.4 us  [body(): all_gates = lax.all_gather(dense_gates, 'ep', axis=0, tiled=True)]
    unnamed x17 -> x6, local copies, waits for them, and re-layouts: 14.3 us -> 3.19 us
    ppermute x0 -> x3, waiting for transfers between devices: none -> 9.27 us  [the longest x2 9.26 us: ring_gather(): from_left = lax.ppermute(from_left, axis, right)]
  transfers between devices with their start and end apart: 8 -> 10, of which waited for: 8 -> 8; matrix products, arithmetic and copies ran while one was open for 5% -> 9% of each run, Pallas kernels for 0% -> 0%
where the time goes in v1:
time: 489 us
  waiting for transfers between devices  408 us (83%)
  matrix products  38.8 us (8%)
  blocking collectives  18.4 us (4%)
  between operations  14.2 us (3%)
  local copies, waits for them, and re-layouts  6.11 us (1%)
    reduce_scatter x1, waiting for transfers between devices, body(): lax.psum_scatter(contract_first(rows, d_pre).astype(bf16), 'fsdp', scatte...  99.5 us
    reduce_scatter x1, waiting for transfers between devices, body(): lax.psum_scatter(contract_first(hidden, grad_rows).astype(bf16), 'fsdp',...  99.3 us
    all_gather x1, waiting for transfers between devices, body(): down = lax.all_gather(down_weight, 'fsdp', axis=1, tiled=True)[0]  74.1 us
    all_gather x1, waiting for transfers between devices, body(): up = lax.all_gather(up_weight, 'fsdp', axis=1, tiled=True)[0]  49 us
    reduce_scatter x1, waiting for transfers between devices, body(): token_grad = lax.psum_scatter(back, 'ep', scatter_dimension=0, tiled=True)  41.1 us
    all_gather x1, waiting for transfers between devices, body(): cot = lax.all_gather(cotangent, 'ep', axis=0, tiled=True)  21 us
    all_gather x1, blocking collectives, body(): all_gates = lax.all_gather(dense_gates, 'ep', axis=0, tiled=True)  18.4 us
    dot_general x2, matrix products, contract_last(): lax.dot_general(left, right, (((1,), (1,)), ((), ())), preferred_element_...  13.6 us
  transfers between devices with their start and end apart: 10, of which 8 were waited for; matrix products, arithmetic and copies ran while one was open for 9% of the time, Pallas kernels for 0%

profile of v1, /device:TPU:0, one launch (start us, length us, event | category | flops | bytes accessed | tf_op | source)
XLA Modules:
  0.0 489.0 jit_solution(11620797197155897777)
XLA Ops:
  7.2 0.7 all-gather.4.cloned.1.call-update
  7.9 0.7 all-gather.6.cloned.1.call-update
  8.7 0.7 all-gather.8.cloned.1.call-update
  9.4 0.5 collective-permute-start
  9.9 2.0 collective-permute-start.1
  11.9 0.8 select_reduce_fusion.1
  12.7 18.4 %all_gather.14 = f32[512,4]{0,1:T(4,128)S(1)} all-gather(f32[128,4]{0,1:T(4,128)S(1)} %select_reduce_fusion.1), channel_id=1, replica_groups=mesh['fsdp'=8,'ep'=4] {'ep'}, dimensions={0}, use_global_device_ids=true | all-gather | bytes 10240 | tf_op jit(solution)/shard_map/all_gather | solution.py:57
  31.1 0.4 broadcast_in_dim.38
  31.5 0.1 constant_dynamic-update-slice_fusion.3
  31.6 0.4 collective-permute-start.2
  31.9 0.1 select_reduce_fusion
  32.0 1.2 constant_dynamic-update-slice_fusion.2
  33.3 1.2 constant_dynamic-update-slice_fusion.1
  34.5 9.3 %collective-permute-done.2 = bf16[128,3072]{1,0:T(8,128)(2,1)S(1)} collective-permute-done((bf16[128,3072]{1,0:T(8,128)(2,1)}, bf16[128,3072]{1,0:T(8,128)(2,1)S(1)}, u32[]{:S(2)}, u32[]{:S(2)}) %collective-permute-start.2) | collective-permute-done | bytes 786464 | tf_op jit(solution)/shard_map/ppermute | solution.py:16
  43.7 0.1 constant_dynamic-update-slice_fusion
  43.8 49.0 %all-gather.4.cloned.1.call-done = bf16[1,3072,768]{2,1,0:T(8,128)(2,1)} async-done(((bf16[1,384,768]{2,1,0:T(8,128)(2,1)}), bf16[1,3072,768]{2,1,0:T(8,128)(2,1)}) %all-gather.4.cloned.1.call-update) | async-done | bytes 4718608 | tf_op jit(solution)/shard_map/all_gather | solution.py:61
  92.8 6.1 %fusion.5 = f32[512,768]{1,0:T(8,128)} fusion(bf16[512,3072]{1,0:T(8,128)(2,1)S(1)} %constant_dynamic-update-slice_fusion, bf16[1,3072,768]{2,1,0:T(8,128)(2,1)} %all-gather.4.cloned.1.call-done), kind=kOutput, calls=%fused_computation.9 | convolution fusion | flops 2415919104 | bytes 9437184 | tf_op jit(solution)/shard_map/dot_general | solution.py:65
  98.9 74.1 %all-gather.6.cloned.1.call-done = bf16[1,768,3072]{2,1,0:T(8,128)(2,1)} async-done(((bf16[1,96,3072]{2,1,0:T(8,128)(2,1)}), bf16[1,768,3072]{2,1,0:T(8,128)(2,1)}) %all-gather.6.cloned.1.call-update) | async-done | bytes 4718608 | tf_op jit(solution)/shard_map/all_gather | solution.py:63
  173.0 7.2 %multiply_convert_fusion.1 = bf16[512,3072]{1,0:T(8,128)(2,1)} fusion(bf16[1,768,3072]{2,1,0:T(8,128)(2,1)} %all-gather.6.cloned.1.call-done, f32[512]{0:T(512)S(1)} %select_reduce_fusion, f32[512,768]{1,0:T(8,128)} %fusion.5), kind=kOutput, calls=%fused_computation.1 | convolution fusion | flops 2422603776 | bytes 9439232 | tf_op jit(solution)/shard_map/dot_general | solution.py:76
  180.3 0.0 reduce-scatter.7.cloned.1.call-start
  180.3 21.0 %all-gather.8.cloned.1.call-done = bf16[512,3072]{1,0:T(8,128)(2,1)} async-done(((bf16[128,3072]{1,0:T(8,128)(2,1)}), bf16[512,3072]{1,0:T(8,128)(2,1)}) %all-gather.8.cloned.1.call-update) | async-done | bytes 3145744 | tf_op jit(solution)/shard_map/all_gather | solution.py:62
  201.3 7.0 %fusion.16 = bf16[512,768]{1,0:T(8,128)(2,1)S(1)} fusion(f32[512,768]{1,0:T(8,128)} %fusion.5, bf16[1,768,3072]{2,1,0:T(8,128)(2,1)} %all-gather.6.cloned.1.call-done, bf16[512,3072]{1,0:T(8,128)(2,1)} %all-gather.8.cloned.1.call-done, f32[512]{0:T(512)S(1)} %select_reduce_fusion), kind=kOutput, calls=%fused_computation.20 | convolution fusion | flops 2428108800 | bytes 10225664 | tf_op jit(solution)/shard_map/dot_general | solution.py:40
  208.3 0.9 copy-done.2
  209.2 6.5 %fusion.7 = bf16[512,3072]{1,0:T(8,128)(2,1)} fusion(bf16[512,768]{1,0:T(8,128)(2,1)S(1)} %fusion.16, bf16[1,3072,768]{2,1,0:T(8,128)(2,1)} %all-gather.4.cloned.1.call-done), kind=kOutput, calls=%fused_computation.11 | convolution fusion | flops 2417491968 | bytes 8650752 | tf_op jit(solution)/shard_map/dot_general | solution.py:40
  215.8 0.0 reduce-scatter.9.cloned.1.call-start
  215.9 5.5 %convolution_convert_fusion.1 = bf16[3072,768]{1,0:T(8,128)(2,1)} fusion(bf16[512,3072]{1,0:T(8,128)(2,1)S(1)} %constant_dynamic-update-slice_fusion, bf16[512,768]{1,0:T(8,128)(2,1)} %copy-done.2), kind=kOutput, calls=%fused_computation.3 | convolution fusion | flops 2418278400 | bytes 8650752 | tf_op jit(solution)/shard_map/dot_general | solution.py:46
  221.4 2.3 copy-done.1
  223.7 6.4 %convolution_convert_fusion = bf16[768,3072]{1,0:T(8,128)(2,1)} fusion(bf16[512,3072]{1,0:T(8,128)(2,1)S(1)} %copy-done.1, f32[512]{0:T(512)S(1)} %select_reduce_fusion, f32[512,768]{1,0:T(8,128)} %fusion.5), kind=kOutput, calls=%fused_computation.2 | convolution fusion | flops 2426535936 | bytes 9439232 | tf_op jit(solution)/shard_map/dot_general | solution.py:46
  230.1 12.1 %reduce-scatter.5.cloned.1.call-done = bf16[128,3072]{1,0:T(8,128)(2,1)} async-done(((bf16[512,3072]{1,0:T(8,128)(2,1)}), bf16[128,3072]{1,0:T(8,128)(2,1)}) %reduce-scatter.5.cloned.1.call-update) | async-done | bytes 786448 | tf_op jit(solution)/shard_map/reduce_scatter | solution.py:77
  242.3 41.1 %reduce-scatter.7.cloned.1.call-done = bf16[128,3072]{1,0:T(8,128)(2,1)} async-done(((bf16[512,3072]{1,0:T(8,128)(2,1)}), bf16[128,3072]{1,0:T(8,128)(2,1)}) %reduce-scatter.7.cloned.1.call-update) | async-done | bytes 786448 | tf_op jit(solution)/shard_map/reduce_scatter | solution.py:79
  283.4 99.5 %reduce-scatter.9.cloned.1.call-done = bf16[384,768]{1,0:T(8,128)(2,1)} async-done(((bf16[3072,768]{1,0:T(8,128)(2,1)}), bf16[384,768]{1,0:T(8,128)(2,1)}) %reduce-scatter.9.cloned.1.call-update) | async-done | bytes 589840 | tf_op jit(solution)/shard_map/reduce_scatter | solution.py:73
  382.9 99.3 %reduce-scatter.11.cloned.1.call-done = bf16[96,3072]{1,0:T(8,128)(2,1)} async-done(((bf16[768,3072]{1,0:T(8,128)(2,1)}), bf16[96,3072]{1,0:T(8,128)(2,1)}) %reduce-scatter.11.cloned.1.call-update) | async-done | bytes 589840 | tf_op jit(solution)/shard_map/reduce_scatter | solution.py:68
  (16 shorter events, 0.3 us)
Async XLA Ops:
  7.2 85.6 %all-gather.4.cloned.1.call-start = ((), (), s32[]{:S(2)}) async-start(), calls=%async_computation.4 | async-start | bytes 5308416 | tf_op jit(solution)/shard_map/all_gather | solution.py:61
  7.9 165.1 %all-gather.6.cloned.1.call-start = ((), (), s32[]{:S(2)}) async-start(), calls=%async_computation.5 | async-start | bytes 5308416 | tf_op jit(solution)/shard_map/all_gather | solution.py:63
  8.6 192.7 %all-gather.8.cloned.1.call-start = ((), (), s32[]{:S(2)}) async-start(), calls=%async_computation.7 | async-start | bytes 3932160 | tf_op jit(solution)/shard_map/all_gather | solution.py:62
  9.4 232.9 %reduce-scatter.5.cloned.1.call-start = ((), (), s32[]{:S(2)}) async-start(), calls=%async_computation.6 | async-start | bytes 3932160 | tf_op jit(solution)/shard_map/reduce_scatter | solution.py:77
  9.4 22.2 %collective-permute-start = (bf16[128,3072]{1,0:T(8,128)(2,1)}, bf16[128,3072]{1,0:T(8,128)(2,1)}, u32[]{:S(2)}, u32[]{:S(2)}) collective-permute-start(bf16[128,3072]{1,0:T(8,128)(2,1)} %param.6), channel_id=1, source_target_pairs={{0,1},{1,2},{2,3},{3,0},{4,5},{5,6},{6,7},{7,4},{8,9},{9,10},{10,1... | collective-permute-start | bytes 2359304 | tf_op jit(solution)/shard_map/ppermute | solution.py:16
  9.9 23.3 %collective-permute-start.1 = (bf16[128,3072]{1,0:T(8,128)(2,1)}, bf16[128,3072]{1,0:T(8,128)(2,1)}, u32[]{:S(2)}, u32[]{:S(2)}) collective-permute-start(bf16[128,3072]{1,0:T(8,128)(2,1)} %param.6), channel_id=1, source_target_pairs={{0,3},{1,0},{2,1},{3,2},{4,7},{5,4},{6,5},{7,6},{8,11},{9,8},{10,9... | collective-permute-start | bytes 2359304 | tf_op jit(solution)/shard_map/ppermute | solution.py:21
  11.9 19.6 %copy-start = (bf16[128,3072]{1,0:T(8,128)(2,1)S(1)}, bf16[128,3072]{1,0:T(8,128)(2,1)}, u32[]{:S(2)}) copy-start(bf16[128,3072]{1,0:T(8,128)(2,1)} %param.6) | copy-start | bytes 2359300
  31.6 12.1 %collective-permute-start.2 = (bf16[128,3072]{1,0:T(8,128)(2,1)}, bf16[128,3072]{1,0:T(8,128)(2,1)S(1)}, u32[]{:S(2)}, u32[]{:S(2)}) collective-permute-start(bf16[128,3072]{1,0:T(8,128)(2,1)} %collective-permute-done), channel_id=1, source_target_pairs={{0,1},{1,2},{2,3},{3,0},{4,5},{5,6},{6,7},{7,4},{8,9},{9,10},{10,1... | collective-permute-start | bytes 2359304 | tf_op jit(solution)/shard_map/ppermute | solution.py:16
  180.3 103.1 %reduce-scatter.7.cloned.1.call-start = ((), (), s32[]{:S(2)}) async-start(), calls=%async_computation.8 | async-start | bytes 3932160 | tf_op jit(solution)/shard_map/reduce_scatter | solution.py:79
  208.3 0.9 copy-start.2
  215.8 167.1 %reduce-scatter.9.cloned.1.call-start = ((), (), s32[]{:S(2)}) async-start(), calls=%async_computation.9 | async-start | bytes 5308416 | tf_op jit(solution)/shard_map/reduce_scatter | solution.py:73
  221.3 2.3 copy-start.1
  221.4 260.8 %reduce-scatter.11.cloned.1.call-start = ((), (), s32[]{:S(2)}) async-start(), calls=%async_computation.10 | async-start | bytes 5308416 | tf_op jit(solution)/shard_map/reduce_scatter | solution.py:68
Sparse Core Ops, SparseCore 0:
  10.2 82.5 all-gather.3
  95.0 78.0 all-gather.5
  174.6 26.6 all-gather.7
  204.3 37.9 reduce-scatter.4
  245.4 37.9 reduce-scatter.6
  287.5 95.4 reduce-scatter.8
  387.1 94.9 reduce-scatter.10
